TPU v7x, 768 devices: a whole 4x8x12 slice. The times are simulated.
768 devices in a mesh: tile: 96 (over z, y), mode: 8 (over x, core).
Axes of the slice: x: 4, y: 8, z: 12, core: 2. Of those that a mesh axis runs over, the one named last changes fastest.
Arguments:
- intensity: float32 [192, 256, 256], P('tile'), may hold values from 0.05 to 4
- positions: int32 [192, 2], replicated, may hold values from 0 to 24575, as said below
- object_field: float32 [2, 320, 24576], P(None, None, 'tile'), may hold values from -4 to 4
- probe_modes: float32 [8, 2, 256, 256], P('mode'), may hold values from -1.5 to 1.5
- kernel_taps: float32 [2, 129], replicated, may hold values from -0.375 to 0.375
Outputs:
- new_object: float32 [2, 320, 24576], P(None, None, 'tile')
Inputs may be any that keep to these rules, and one draw needn't show every extreme that they name: `positions`: pattern g belongs to scan block b = g // 2; its centre column lies in tile b - 1, b or b + 1, tile t holding columns t * 256 to (t + 1) * 256 - 1. From one block at most 1 patterns lie in each neighbouring tile; in every draw some block has 1 in its right neighbour and some block 1 in its left neighbour, and some tile keeps all 2 of its own block and gets 1 from each neighbouring block. Within its tile, the centre column of an even-numbered pattern of a block lies in the last 64 columns, that of an odd-numbered one in the first 64 columns. Rows lie in 0 to 64.
All inputs are finite; a program needn't handle non-finite values.
Results may differ from a plain program's by a relative error of at most 0.0023.
Values sent between devices are 32-bit elements; how exact they have to be, the bound alone decides.
No kernel may reach another device: no remote copies, remote signals or barrier semaphores. Data moves between devices by JAX's collectives and lax.ppermute only.
A program may use at most 32 MiB of HBM per device.

v0:
```python
import functools

import jax
import jax.numpy as jnp
from jax import lax
from jax.experimental import pallas as pl
from jax.experimental.pallas import tpu as pltpu
from jax.sharding import PartitionSpec as P

P_SIZE = 256
BAND = 64
TW = 256
HALF = 128
OH = 320
MODES = 8
EXT = TW + HALF
TALL = P_SIZE + 8
GROUP = 4
HELD = MODES // 2
REACH = P_SIZE - BAND
F32 = jnp.float32
BF16 = jnp.bfloat16


def place_of(tiles):
    return lax.axis_index("tile"), lax.rem(lax.axis_index("mode"), 2)


def slot_of(pos_ref, tile, core, tiles, shift):
    block = tile + shift
    inside = (block >= 0) & (block < tiles)
    pattern = 2 * jnp.clip(block, 0, tiles - 1) + core
    return inside, pos_ref[0, pattern], pos_ref[1, pattern]


def aligned(top_row):
    extra = lax.rem(top_row, 8)
    return pl.multiple_of(top_row - extra, 8), extra


def lowered(window, extra, width):
    tall = jnp.concatenate([window, jnp.zeros((TALL - P_SIZE, P_SIZE), F32)], axis=0)
    return jnp.concatenate([pltpu.roll(tall, extra, 0), jnp.zeros((TALL, width - P_SIZE), F32)], axis=1)


def run_copies(moves, sem):
    copies = [pltpu.make_async_copy(src, dst, sem.at[i]) for i, (src, dst) in enumerate(moves)]
    for copy in copies:
        copy.start()
    for copy in copies:
        copy.wait()


def pack_kernel(obj, own, halo, merged, sem):
    core = lax.rem(lax.axis_index("mode"), 2)
    edge = pl.ds(pl.multiple_of(core * HALF, HALF), HALF)
    run_copies([(obj.at[:, :, edge], halo), (own.at[0], merged.at[0:2])], sem)


def merge_kernel(before, first, second, third, merged, sem):
    del before
    arrays = (first, second, third)
    run_copies([(array.at[0], merged.at[2 * i + 2 : 2 * i + 4]) for i, array in enumerate(arrays)], sem)


def append_kernel(inward, before, merged, sem):
    del before
    core = lax.rem(lax.axis_index("mode"), 2)
    run_copies([(inward.at[1 - core], merged.at[MODES])], sem)


def window_of(pos_ref, tiles, slot):
    tile, core = place_of(tiles)
    inside, top_row, column = slot_of(pos_ref, tile, core, tiles, (slot - 1) * (1 - 2 * core))
    offset = column - tile * TW - (1 - core) * HALF
    here = inside & (column >= tile * TW) & (column < (tile + 1) * TW)
    return here, top_row, offset


def columns_of(unit):
    return slice(unit * P_SIZE, (unit + 1) * P_SIZE)


def put_split(low, own, value_re, value_im):
    low[:HALF, own] = value_re[:HALF].astype(BF16)
    low[HALF : 2 * HALF, own] = value_im[:HALF].astype(BF16)
    low[2 * HALF : 3 * HALF, own] = value_re[HALF:].astype(BF16)
    low[3 * HALF :, own] = value_im[HALF:].astype(BF16)


def mix(left, second, low, midb):
    upper = jnp.dot(left[0], low[: 2 * HALF], preferred_element_type=F32)
    lower = jnp.dot(left[1], low[2 * HALF :], preferred_element_type=F32)
    for unit in range(GROUP):
        own = columns_of(unit)
        first_row = unit * P_SIZE
        for part in range(2):
            to = slice(part * P_SIZE, (part + 1) * P_SIZE)
            up = upper[part * REACH : (part + 1) * REACH, own]
            down = lower[part * REACH : (part + 1) * REACH, own]
            midb[first_row : first_row + BAND, to] = up[:BAND].astype(BF16)
            midb[first_row + BAND : first_row + REACH, to] = (up[BAND:] + down[: REACH - BAND]).astype(BF16)
            midb[first_row + REACH : first_row + P_SIZE, to] = down[REACH - BAND :].astype(BF16)
    return jnp.dot(midb[...], second, preferred_element_type=F32)


def forward(probe, modes, patch_re, patch_im, left, stacks, low, midb, far, power):
    for unit, mode in enumerate(modes):
        pr = probe[2 * mode]
        pi = probe[2 * mode + 1]
        re, im = patch_re[...], patch_im[...]
        put_split(low, columns_of(unit), pr * re - pi * im, pr * im + pi * re)
    out = mix(left.at[0], stacks[1], low, midb)
    for unit in range(len(modes)):
        block = out[columns_of(unit)]
        far[unit] = block
        power[...] += block[:, :P_SIZE] * block[:, :P_SIZE] + block[:, P_SIZE:] * block[:, P_SIZE:]


def first_kernel(tiles, pos_ref, taps_ref, obj, beside, mine, patch, left, stacks, far, power, wave, low, midb, row_pad, sem):
    _, core = place_of(tiles)
    rim = pl.ds(pl.multiple_of((1 - core) * TW, HALF), HALF)
    moves = (
        (obj, wave.at[:, :OH, pl.ds(pl.multiple_of(core * HALF, HALF), TW)]),
        (beside, wave.at[:, :OH, rim]),
    )
    copies = [pltpu.make_async_copy(src, dst, sem.at[i]) for i, (src, dst) in enumerate(moves)]
    for copy in copies:
        copy.start()

    row_pad[...] = jnp.zeros_like(row_pad)
    row_pad[0:2, 0 : 2 * BAND + 1] = taps_ref[...]

    def band(part):
        line = jnp.broadcast_to(row_pad[part : part + 1, :], (P_SIZE, 2 * P_SIZE))
        turned = pltpu.roll(line, 2 * P_SIZE - BAND, 1, stride=1, stride_axis=0)
        return turned[:, :P_SIZE]

    band_re = band(0)
    band_im = band(1)
    turned_re = band_re.T
    turned_im = band_im.T
    for which, blocks in enumerate(((band_re, -band_im, band_im), (turned_re, turned_im, -turned_im))):
        stacks[which, :P_SIZE, :P_SIZE] = blocks[0].astype(BF16)
        stacks[which, :P_SIZE, P_SIZE:] = blocks[1].astype(BF16)
        stacks[which, P_SIZE:, :P_SIZE] = blocks[2].astype(BF16)
        stacks[which, P_SIZE:, P_SIZE:] = blocks[0].astype(BF16)
        for half in range(2):
            rows = slice(half * BAND, half * BAND + REACH)
            part = slice(half * HALF, (half + 1) * HALF)
            left[which, half, :REACH, :HALF] = blocks[0][rows, part].astype(BF16)
            left[which, half, :REACH, HALF:] = blocks[1][rows, part].astype(BF16)
            left[which, half, REACH:, :HALF] = blocks[2][rows, part].astype(BF16)
            left[which, half, REACH:, HALF:] = blocks[0][rows, part].astype(BF16)

    for copy in copies:
        copy.wait()

    @pl.loop(0, 3)
    def _(slot):
        here, top_row, offset = window_of(pos_ref, tiles, slot)

        @pl.when(here)
        def _():
            base, extra = aligned(top_row)
            for part in range(2):
                rows = wave[part, pl.ds(base, TALL), :]
                turned = pltpu.roll(rows, lax.rem(EXT - offset, EXT), 1)[:, :P_SIZE]
                patch[slot, part] = pltpu.roll(turned, lax.rem(TALL - extra, TALL), 0)[:P_SIZE]
            power[slot] = jnp.zeros((P_SIZE, P_SIZE), F32)
            sides = (patch.at[slot, 0], patch.at[slot, 1])
            forward(mine, range(GROUP), *sides, left, stacks, low.at[0], midb.at[0], far.at[slot], power.at[slot])


def second_kernel(
    tiles, pos_ref, inten, inward, mine, theirs, far, patch, power, left, stacks, mid_out, rim_out, weight,
    total, meas, far_too, low, midb, ratio, acc,
):
    _, core = place_of(tiles)
    total[...] = jnp.zeros_like(total)
    meas[0] = theirs[MODES]
    meas[1] = inten[core]
    meas[2] = inward[core]
    weight[...] = jnp.zeros_like(weight)

    @pl.loop(0, MODES)
    def _(plane):
        weight[...] += mine[plane] * mine[plane] + theirs[plane] * theirs[plane]

    @pl.loop(0, 3)
    def _(slot):
        here, top_row, offset = window_of(pos_ref, tiles, slot)

        @pl.when(here)
        def _():
            base, extra = aligned(top_row)
            ratio[...] = power[slot]
            sides = (patch.at[slot, 0], patch.at[slot, 1])
            forward(theirs, range(GROUP), *sides, left, stacks, low.at[0], midb.at[0], far_too, ratio)
            ratio[...] = jnp.sqrt(meas[slot]) / jnp.sqrt(ratio[...] + 1.0)
            acc[0] = -weight[...] * patch[slot, 0]
            acc[1] = -weight[...] * patch[slot, 1]
            fields = [(far.at[slot, i], mine, i) for i in range(HELD)]
            fields += [(far_too.at[i], theirs, i) for i in range(HELD)]
            for start in range(0, MODES, GROUP):
                group = fields[start : start + GROUP]
                turn = start // GROUP % 2
                for unit, (source, _, _) in enumerate(group):
                    scaled = ratio[...]
                    put_split(low.at[turn], columns_of(unit), source[:, :P_SIZE] * scaled, source[:, P_SIZE:] * scaled)
                out = mix(left.at[1], stacks[0], low.at[turn], midb.at[turn])
                term_re = 0.0
                term_im = 0.0
                for unit, (_, probe, mode) in enumerate(group):
                    back_re = out[columns_of(unit), :P_SIZE]
                    back_im = out[columns_of(unit), P_SIZE:]
                    pr = probe[2 * mode]
                    pi = probe[2 * mode + 1]
                    term_re += pr * back_re + pi * back_im
                    term_im += pr * back_im - pi * back_re
                acc[0] += term_re
                acc[1] += term_im

            for part in range(2):
                total[part, pl.ds(base, TALL), :] += pltpu.roll(lowered(acc[part], extra, EXT), offset, 1)

    mid_out[...] = total[:, :OH, pl.ds(pl.multiple_of(core * HALF, HALF), TW)]
    rim_out[...] = total[:, :OH, pl.ds(pl.multiple_of((1 - core) * TW, HALF), HALF)]


def denom_kernel(tiles, pos_ref, weight, scale, denom):
    tile, _ = place_of(tiles)
    denom[...] = jnp.zeros_like(denom)
    for parity, shifts in ((0, (-2, -1, 0, 1)), (1, (-1, 0, 1, 2))):
        for shift in shifts:
            inside, top_row, column = slot_of(pos_ref, tile, parity, tiles, shift)
            start = column - HALF - tile * TW

            @pl.when(inside & (start > -P_SIZE) & (start < TW))
            def _():
                base, extra = aligned(top_row)
                wide = lowered(weight[...], extra, 2 * P_SIZE)
                turned = pltpu.roll(wide, jnp.where(start < 0, start + 2 * P_SIZE, start), 1)
                denom[pl.ds(base, TALL), :] += turned[:, :TW]

    scale[...] = 1.0 / (denom[:OH] + 0.5)


ANY = pl.BlockSpec(memory_space=pl.ANY)
HBM = pl.BlockSpec(memory_space=pltpu.HBM)
VMEM = pl.BlockSpec(memory_space=pltpu.VMEM)
SMEM = pl.BlockSpec(memory_space=pltpu.SMEM)


def f32(*shape):
    return jax.ShapeDtypeStruct(shape, F32)


def limit(mib):
    return pltpu.CompilerParams(vmem_limit_bytes=mib * 2**20)


def cost(us):
    return pl.CostEstimate(flops=0, bytes_accessed=int(us * 3.5e6), transcendentals=0)


def local(intensity, positions, object_field, probe_modes, kernel_taps):
    tiles = lax.axis_size("tile")
    modes = lax.axis_size("mode")
    core = lax.rem(lax.axis_index("mode"), 2)
    spots = positions.T

    def along_x(array, steps):
        return lax.ppermute(array, "mode", [(i, (i + 2 * steps) % modes) for i in range(modes)])

    def swap(array):
        return lax.ppermute(array, "mode", [(i, i ^ 1) for i in range(modes)])

    def from_tile(array, step):
        pairs = []
        for tile in range(tiles):
            for mode in range(modes):
                source = tile + step if mode % 2 == 0 else tile - step
                if 0 <= source < tiles:
                    pairs.append((source * modes + mode, tile * modes + mode))
        return lax.ppermute(array, ("tile", "mode"), pairs)

    ring = [along_x(probe_modes, step) for step in (2, 1, -1)]
    edge, held = pl.pallas_call(
        pack_kernel,
        out_shape=(f32(2, OH, HALF), f32(MODES + 1, P_SIZE, P_SIZE)),
        in_specs=[ANY, ANY],
        out_specs=(VMEM, VMEM),
        scratch_shapes=[pltpu.SemaphoreType.DMA((2,))],
        compiler_params=limit(4),
        cost_estimate=cost(2.2),
        name="pack",
    )(object_field, probe_modes)
    beside = from_tile(edge, 1)
    inward = from_tile(intensity, 1)

    def stages(units):
        return [
            pltpu.VMEM((2, 2 * P_SIZE, units * P_SIZE), BF16),
            pltpu.VMEM((2, units * P_SIZE, 2 * P_SIZE), BF16),
        ]

    mine = pl.pallas_call(
        merge_kernel,
        out_shape=f32(MODES + 1, P_SIZE, P_SIZE),
        in_specs=[ANY] * 4,
        out_specs=ANY,
        scratch_shapes=[pltpu.SemaphoreType.DMA((3,))],
        input_output_aliases={0: 0},
        compiler_params=limit(4),
        cost_estimate=cost(1.0),
        name="merge",
    )(held, *ring)
    mine = pl.pallas_call(
        append_kernel,
        out_shape=f32(MODES + 1, P_SIZE, P_SIZE),
        in_specs=[ANY, ANY],
        out_specs=ANY,
        scratch_shapes=[pltpu.SemaphoreType.DMA((1,))],
        input_output_aliases={1: 0},
        compiler_params=limit(4),
        name="append",
    )(inward, mine)
    mine, beside = lax.optimization_barrier((mine, beside))
    theirs = swap(mine)

    patch, left, stacks, far, power = pl.pallas_call(
        functools.partial(first_kernel, tiles),
        out_shape=(
            f32(3, 2, P_SIZE, P_SIZE),
            jax.ShapeDtypeStruct((2, 2, 2 * REACH, 2 * HALF), BF16),
            jax.ShapeDtypeStruct((2, 2 * P_SIZE, 2 * P_SIZE), BF16),
            f32(3, HELD, P_SIZE, 2 * P_SIZE),
            f32(3, P_SIZE, P_SIZE),
        ),
        in_specs=[SMEM, VMEM, ANY, ANY, VMEM],
        out_specs=(VMEM,) * 5,
        scratch_shapes=[pltpu.VMEM((2, OH + 8, EXT), F32)]
        + stages(GROUP)
        + [pltpu.VMEM((8, 2 * P_SIZE), F32), pltpu.SemaphoreType.DMA((2,))],
        compiler_params=limit(16),
        cost_estimate=cost(6.0),
        name="far_of_own_modes",
    )(spots, kernel_taps, object_field, beside, mine)

    middle, rim, weight = pl.pallas_call(
        functools.partial(second_kernel, tiles),
        out_shape=(f32(2, OH, TW), f32(2, OH, HALF), f32(P_SIZE, P_SIZE)),
        in_specs=[SMEM] + [VMEM] * 9,
        out_specs=(VMEM,) * 3,
        scratch_shapes=[
            pltpu.VMEM((2, OH + 8, EXT), F32),
            pltpu.VMEM((3, P_SIZE, P_SIZE), F32),
            pltpu.VMEM((HELD, P_SIZE, 2 * P_SIZE), F32),
        ]
        + stages(GROUP)
        + [pltpu.VMEM((P_SIZE, P_SIZE), F32), pltpu.VMEM((2, P_SIZE, P_SIZE), F32)],
        compiler_params=limit(20),
        cost_estimate=cost(10.0),
        name="update_terms",
    )(spots, intensity, inward, mine, theirs, far, patch, power, left, stacks)

    arrived = from_tile(rim, -1)
    scale = pl.pallas_call(
        functools.partial(denom_kernel, tiles),
        out_shape=f32(OH, TW),
        in_specs=[SMEM, VMEM],
        out_specs=VMEM,
        scratch_shapes=[pltpu.VMEM((OH + 8, TW), F32)],
        compiler_params=limit(4),
        cost_estimate=cost(3.5),
        name="denominator",
    )(spots, weight)
    blank = jnp.zeros_like(arrived)
    low = jnp.where(core == 0, arrived, blank)
    high = jnp.where(core == 0, blank, arrived)
    terms = (middle + jnp.concatenate([low, high], axis=2)) * scale
    return object_field + (terms + swap(terms))


def solution(mesh):
    return jax.shard_map(
        local,
        mesh=mesh,
        in_specs=(
            P("tile", None, None),
            P(),
            P(None, None, "tile"),
            P("mode", None, None, None),
            P(),
        ),
        out_specs=P(None, None, "tile"),
        check_vma=False,
    )
```

profile of v0, /device:TPU:257, one launch (start us, length us, event | category | flops | bytes accessed | tf_op | source)
XLA Modules:
  0.0 62.7 jit_solution(4606455523876187904)
XLA Ops:
  0.0 4.6 %collective-permute-start.1 = (f32[1,2,256,256]{3,2,1,0:T(8,128)}, f32[1,2,256,256]{3,2,1,0:T(8,128)S(1)}, u32[]{:S(2)}, u32[]{:S(2)}) collective-permute-start(f32[1,2,256,256]{3,2,1,0:T(8,128)} %own.1), channel_id=1, source_target_pairs={{0,4},{1,5},{2,6},{3,7},{4,0},{5,1},{6,2},{7,3},{8,12},{9,13},{10,... | collective-permute-start | bytes 1572872 | tf_op jit(solution)/shard_map/ppermute | solution.py:274
  4.6 2.2 %collective-permute-start.2 = (f32[1,2,256,256]{3,2,1,0:T(8,128)}, f32[1,2,256,256]{3,2,1,0:T(8,128)S(1)}, u32[]{:S(2)}, u32[]{:S(2)}) collective-permute-start(f32[1,2,256,256]{3,2,1,0:T(8,128)} %own.1), channel_id=1, source_target_pairs={{0,2},{1,3},{2,4},{3,5},{4,6},{5,7},{6,0},{7,1},{8,10},{9,11},{10,... | collective-permute-start | bytes 1572872 | tf_op jit(solution)/shard_map/ppermute | solution.py:274
  6.9 4.3 %collective-permute-start.3 = (f32[1,2,256,256]{3,2,1,0:T(8,128)}, f32[1,2,256,256]{3,2,1,0:T(8,128)S(1)}, u32[]{:S(2)}, u32[]{:S(2)}) collective-permute-start(f32[1,2,256,256]{3,2,1,0:T(8,128)} %own.1), channel_id=1, source_target_pairs={{0,6},{1,7},{2,0},{3,1},{4,2},{5,3},{6,4},{7,5},{8,14},{9,15},{10,... | collective-permute-start | bytes 1572872 | tf_op jit(solution)/shard_map/ppermute | solution.py:274
  11.2 3.2 %collective-permute-start = (f32[2,256,256]{2,1,0:T(8,128)}, f32[2,256,256]{2,1,0:T(8,128)S(1)}, u32[]{:S(2)}, u32[]{:S(2)}) collective-permute-start(f32[2,256,256]{2,1,0:T(8,128)} %inten.1), channel_id=1, source_target_pairs={{8,0},{10,2},{12,4},{14,6},{16,8},{1,9},{18,10},{3,11},{20,12},{5,... | collective-permute-start | bytes 1572872 | tf_op jit(solution)/shard_map/ppermute | solution.py:286
  14.4 0.0 copy-start
  14.4 1.1 %copy-done = f32[2,320,256]{2,1,0:T(8,128)S(1)} copy-done((f32[2,320,256]{2,1,0:T(8,128)S(1)}, f32[2,320,256]{2,1,0:T(8,128)}, u32[]{:S(2)}) %copy-start) | copy-done | bytes 655384
  15.5 1.0 %copy-done.3 = f32[1,2,256,256]{3,2,1,0:T(8,128)S(1)} copy-done((f32[1,2,256,256]{3,2,1,0:T(8,128)S(1)}, f32[1,2,256,256]{3,2,1,0:T(8,128)}, u32[]{:S(2)}) %copy-start.3) | copy-done | bytes 524312
  16.5 0.1 pack.1
  16.6 3.2 %collective-permute-start.4 = (f32[2,320,128]{2,1,0:T(8,128)S(1)}, f32[2,320,128]{2,1,0:T(8,128)S(1)}, u32[]{:S(2)}, u32[]{:S(2)}) collective-permute-start(f32[2,320,128]{2,1,0:T(8,128)S(1)} %get-tuple-element.18), channel_id=1, source_target_pairs={{8,0},{10,2},{12,4},{14,6},{16,8},{1,9},{18,10},{3,11},{20,12},{5,... | collective-permute-start | bytes 983048 | tf_op jit(solution)/shard_map/ppermute | solution.py:286
  19.8 0.0 collective-permute-done.1.first
  19.8 8.9 %collective-permute-done.2.second = f32[1,2,256,256]{3,2,1,0:T(8,128)S(1)} collective-permute-done((f32[1,2,256,256]{3,2,1,0:T(8,128)}, f32[1,2,256,256]{3,2,1,0:T(8,128)S(1)}, u32[]{:S(2)}, u32[]{:S(2)}) %collective-permute-start.2) | collective-permute-done | bytes 524320 | tf_op jit(solution)/shard_map/ppermute | solution.py:274
  28.7 0.0 collective-permute-done.3.third
  28.7 0.1 merge.1.before
  28.8 0.0 copy-start.1
  28.8 0.0 copy-start.4
  28.9 0.0 copy-start.5
  28.9 0.0 collective-permute-done.inward
  28.9 0.0 copy-start.2
  28.9 0.0 collective-permute-done.4.beside
  28.9 2.7 %collective-permute-start.5 = (f32[9,256,256]{2,1,0:T(8,128)S(1)}, f32[9,256,256]{2,1,0:T(8,128)S(1)}, u32[]{:S(2)}, u32[]{:S(2)}) collective-permute-start(f32[9,256,256]{2,1,0:T(8,128)S(1)} %append.1.mine), channel_id=1, source_target_pairs={{0,1},{1,0},{2,3},{3,2},{4,5},{5,4},{6,7},{7,6},{8,9},{9,8},{10,11... | collective-permute-start | bytes 7077896 | tf_op jit(solution)/shard_map/ppermute | solution.py:277
  31.6 0.0 copy-done.1
  31.6 0.0 copy-done.4
  31.6 4.4 %far_of_own_modes.1 = (f32[3,2,256,256]{3,2,1,0:T(8,128)S(1)}, bf16[2,2,384,256]{3,2,1,0:T(8,128)(2,1)S(1)}, bf16[2,512,512]{2,1,0:T(8,128)(2,1)S(1)}, f32[3,4,256,512]{3,2,1,0:T(8,128)S(1)}, f32[3,256,256]{2,1,0:T(8,128)S(1)}) custom-call(s32[2,192]{1,0:T(2,128)S(1)} %bitcast.1, f32[2,129]{1,0:T(2,128)S(1)} %copy-done.5, f32[2,320,256]{2,1,0:T(8,128)S(1)} %copy-done.1, ...), custom_call_target="tpu_custom_call" | custom-call | bytes 21000000 | tf_op jit(solution)/shard_map/far_of_own_modes/pallas_call | solution.py:332
  36.1 0.0 collective-permute-done.5.theirs
  36.1 9.6 %update_terms.1 = (f32[2,320,256]{2,1,0:T(8,128)S(1)}, f32[2,320,128]{2,1,0:T(8,128)S(1)}, f32[256,256]{1,0:T(8,128)S(1)}) custom-call(s32[2,192]{1,0:T(2,128)S(1)} %bitcast.2, f32[2,256,256]{2,1,0:T(8,128)S(1)} %copy-done.2, f32[2,256,256]{2,1,0:T(8,128)S(1)} %collective-permute-done.inward, f32[9,256,256]{2,1,0:T(8,128)S(1)} %append.1.mine, ...), custom_call_target="tpu_custom_call" | custom-call | bytes 35000000 | tf_op jit(solution)/shard_map/update_terms/pallas_call | solution.py:351
  45.6 1.9 %collective-permute-start.6 = (f32[2,320,128]{2,1,0:T(8,128)S(1)}, f32[2,320,128]{2,1,0:T(8,128)S(1)}, u32[]{:S(2)}, u32[]{:S(2)}) collective-permute-start(f32[2,320,128]{2,1,0:T(8,128)S(1)} %get-tuple-element.27), channel_id=1, source_target_pairs={{9,1},{11,3},{13,5},{15,7},{0,8},{17,9},{2,10},{19,11},{4,12},{21,... | collective-permute-start | bytes 983048 | tf_op jit(solution)/shard_map/ppermute | solution.py:286
  47.6 2.2 %denominator.1 = f32[320,256]{1,0:T(8,128)S(1)} custom-call(s32[2,192]{1,0:T(2,128)S(1)} %bitcast.3, f32[256,256]{1,0:T(8,128)S(1)} %get-tuple-element.28.weight), custom_call_target="tpu_custom_call" | custom-call | bytes 12250000 | tf_op jit(solution)/shard_map/denominator/pallas_call | solution.py:369
  49.8 3.7 %collective-permute-done.6 = f32[2,320,128]{2,1,0:T(8,128)S(1)} collective-permute-done((f32[2,320,128]{2,1,0:T(8,128)S(1)}, f32[2,320,128]{2,1,0:T(8,128)S(1)}, u32[]{:S(2)}, u32[]{:S(2)}) %collective-permute-start.6) | collective-permute-done | bytes 327712 | tf_op jit(solution)/shard_map/ppermute | solution.py:286
  53.5 0.1 fusion
  53.6 6.4 %collective-permute-start.7 = (f32[2,320,256]{2,1,0:T(8,128)S(1)}, f32[2,320,256]{2,1,0:T(8,128)S(1)}, u32[]{:S(2)}, u32[]{:S(2)}) collective-permute-start(f32[2,320,256]{2,1,0:T(8,128)S(1)} %fusion), channel_id=1, source_target_pairs={{0,1},{1,0},{2,3},{3,2},{4,5},{5,4},{6,7},{7,6},{8,9},{9,8},{10,11... | collective-permute-start | bytes 1966088 | tf_op jit(solution)/shard_map/ppermute | solution.py:277
  60.0 1.7 %collective-permute-done.7 = f32[2,320,256]{2,1,0:T(8,128)S(1)} collective-permute-done((f32[2,320,256]{2,1,0:T(8,128)S(1)}, f32[2,320,256]{2,1,0:T(8,128)S(1)}, u32[]{:S(2)}, u32[]{:S(2)}) %collective-permute-start.7) | collective-permute-done | bytes 655392 | tf_op jit(solution)/shard_map/ppermute | solution.py:277
  61.8 1.0 %add_add_fusion = f32[2,320,256]{2,1,0:T(8,128)} fusion(f32[2,320,256]{2,1,0:T(8,128)S(1)} %copy-done.1, f32[2,320,256]{2,1,0:T(8,128)S(1)} %fusion, f32[2,320,256]{2,1,0:T(8,128)S(1)} %collective-permute-done.7), kind=kLoop, calls=%fused_computation.2 | loop fusion | flops 327680 | bytes 2621440 | tf_op jit(solution)/shard_map/add | solution.py:383
  (5 shorter events, 0.1 us)
Async XLA Ops:
  0.0 19.8 %collective-permute-start.1 = (f32[1,2,256,256]{3,2,1,0:T(8,128)}, f32[1,2,256,256]{3,2,1,0:T(8,128)S(1)}, u32[]{:S(2)}, u32[]{:S(2)}) collective-permute-start(f32[1,2,256,256]{3,2,1,0:T(8,128)} %own.1), channel_id=1, source_target_pairs={{0,4},{1,5},{2,6},{3,7},{4,0},{5,1},{6,2},{7,3},{8,12},{9,13},{10,... | collective-permute-start | bytes 1572872 | tf_op jit(solution)/shard_map/ppermute | solution.py:274
  4.6 24.0 %collective-permute-start.2 = (f32[1,2,256,256]{3,2,1,0:T(8,128)}, f32[1,2,256,256]{3,2,1,0:T(8,128)S(1)}, u32[]{:S(2)}, u32[]{:S(2)}) collective-permute-start(f32[1,2,256,256]{3,2,1,0:T(8,128)} %own.1), channel_id=1, source_target_pairs={{0,2},{1,3},{2,4},{3,5},{4,6},{5,7},{6,0},{7,1},{8,10},{9,11},{10,... | collective-permute-start | bytes 1572872 | tf_op jit(solution)/shard_map/ppermute | solution.py:274
  6.9 21.8 %collective-permute-start.3 = (f32[1,2,256,256]{3,2,1,0:T(8,128)}, f32[1,2,256,256]{3,2,1,0:T(8,128)S(1)}, u32[]{:S(2)}, u32[]{:S(2)}) collective-permute-start(f32[1,2,256,256]{3,2,1,0:T(8,128)} %own.1), channel_id=1, source_target_pairs={{0,6},{1,7},{2,0},{3,1},{4,2},{5,3},{6,4},{7,5},{8,14},{9,15},{10,... | collective-permute-start | bytes 1572872 | tf_op jit(solution)/shard_map/ppermute | solution.py:274
  11.2 17.7 %collective-permute-start = (f32[2,256,256]{2,1,0:T(8,128)}, f32[2,256,256]{2,1,0:T(8,128)S(1)}, u32[]{:S(2)}, u32[]{:S(2)}) collective-permute-start(f32[2,256,256]{2,1,0:T(8,128)} %inten.1), channel_id=1, source_target_pairs={{8,0},{10,2},{12,4},{14,6},{16,8},{1,9},{18,10},{3,11},{20,12},{5,... | collective-permute-start | bytes 1572872 | tf_op jit(solution)/shard_map/ppermute | solution.py:286
  14.4 1.1 %copy-start = (f32[2,320,256]{2,1,0:T(8,128)S(1)}, f32[2,320,256]{2,1,0:T(8,128)}, u32[]{:S(2)}) copy-start(f32[2,320,256]{2,1,0:T(8,128)} %obj.3) | copy-start | bytes 1966084
  15.5 1.0 %copy-start.3 = (f32[1,2,256,256]{3,2,1,0:T(8,128)S(1)}, f32[1,2,256,256]{3,2,1,0:T(8,128)}, u32[]{:S(2)}) copy-start(f32[1,2,256,256]{3,2,1,0:T(8,128)} %own.1) | copy-start | bytes 1572868
  16.6 12.3 %collective-permute-start.4 = (f32[2,320,128]{2,1,0:T(8,128)S(1)}, f32[2,320,128]{2,1,0:T(8,128)S(1)}, u32[]{:S(2)}, u32[]{:S(2)}) collective-permute-start(f32[2,320,128]{2,1,0:T(8,128)S(1)} %get-tuple-element.18), channel_id=1, source_target_pairs={{8,0},{10,2},{12,4},{14,6},{16,8},{1,9},{18,10},{3,11},{20,12},{5,... | collective-permute-start | bytes 983048 | tf_op jit(solution)/shard_map/ppermute | solution.py:286
  28.8 2.8 %copy-start.1 = (f32[2,320,256]{2,1,0:T(8,128)S(1)}, f32[2,320,256]{2,1,0:T(8,128)}, u32[]{:S(2)}) copy-start(f32[2,320,256]{2,1,0:T(8,128)} %obj.3) | copy-start | bytes 1966084
  28.8 2.8 %copy-start.4 = (s32[192,2]{0,1:T(2,128)S(1)}, s32[192,2]{0,1:T(2,128)}, u32[]{:S(2)}) copy-start(s32[192,2]{0,1:T(2,128)} %param.6) | copy-start | bytes 4612
  28.9 2.8 %copy-start.5 = (f32[2,129]{1,0:T(2,128)S(1)}, f32[2,129]{1,0:T(2,128)}, u32[]{:S(2)}) copy-start(f32[2,129]{1,0:T(2,128)} %taps_ref.1) | copy-start | bytes 3100
  28.9 7.1 %copy-start.2 = (f32[2,256,256]{2,1,0:T(8,128)S(1)}, f32[2,256,256]{2,1,0:T(8,128)}, u32[]{:S(2)}) copy-start(f32[2,256,256]{2,1,0:T(8,128)} %inten.1) | copy-start | bytes 1572868
  28.9 7.1 %collective-permute-start.5 = (f32[9,256,256]{2,1,0:T(8,128)S(1)}, f32[9,256,256]{2,1,0:T(8,128)S(1)}, u32[]{:S(2)}, u32[]{:S(2)}) collective-permute-start(f32[9,256,256]{2,1,0:T(8,128)S(1)} %append.1.mine), channel_id=1, source_target_pairs={{0,1},{1,0},{2,3},{3,2},{4,5},{5,4},{6,7},{7,6},{8,9},{9,8},{10,11... | collective-permute-start | bytes 7077896 | tf_op jit(solution)/shard_map/ppermute | solution.py:277
  45.6 7.8 %collective-permute-start.6 = (f32[2,320,128]{2,1,0:T(8,128)S(1)}, f32[2,320,128]{2,1,0:T(8,128)S(1)}, u32[]{:S(2)}, u32[]{:S(2)}) collective-permute-start(f32[2,320,128]{2,1,0:T(8,128)S(1)} %get-tuple-element.27), channel_id=1, source_target_pairs={{9,1},{11,3},{13,5},{15,7},{0,8},{17,9},{2,10},{19,11},{4,12},{21,... | collective-permute-start | bytes 983048 | tf_op jit(solution)/shard_map/ppermute | solution.py:286
  53.6 8.1 %collective-permute-start.7 = (f32[2,320,256]{2,1,0:T(8,128)S(1)}, f32[2,320,256]{2,1,0:T(8,128)S(1)}, u32[]{:S(2)}, u32[]{:S(2)}) collective-permute-start(f32[2,320,256]{2,1,0:T(8,128)S(1)} %fusion), channel_id=1, source_target_pairs={{0,1},{1,0},{2,3},{3,2},{4,5},{5,4},{6,7},{7,6},{8,9},{9,8},{10,11... | collective-permute-start | bytes 1966088 | tf_op jit(solution)/shard_map/ppermute | solution.py:277
where the time goes:
time: 63.3 us; the launch traced here: 62.7 us
  starting transfers between devices  28.6 us (45%)
  Pallas kernels  16.4 us (26%)
  waiting for transfers between devices  14.3 us (23%)
  local copies, waits for them, and re-layouts  2.15 us (3%)
  other arithmetic  1.1 us (2%)
    ppermute x3, starting transfers between devices, along_x(): lax.ppermute(array, 'mode', [(i, (i + 2 * steps) % modes) for i in range(...  11.1 us
    pallas_call x1, Pallas kernels, local(): pl.pallas_call(functools.partial(second_kernel, tiles), out_shape=(f32(2,...  9.56 us
    ppermute x2, starting transfers between devices, swap(): return lax.ppermute(array, 'mode', [(i, i ^ 1) for i in range(modes)])  9.1 us
    ppermute x3, waiting for transfers between devices, along_x(): lax.ppermute(array, 'mode', [(i, (i + 2 * steps) % modes) for i in range(...  8.87 us
    ppermute x3, starting transfers between devices, from_tile(): return lax.ppermute(array, ('tile', 'mode'), pairs)  8.33 us
    pallas_call x1, Pallas kernels, local(): pl.pallas_call(functools.partial(first_kernel, tiles), out_shape=(f32(3,...  4.4 us
    ppermute x3, waiting for transfers between devices, from_tile(): return lax.ppermute(array, ('tile', 'mode'), pairs)  3.69 us
    pallas_call x1, Pallas kernels, local(): pl.pallas_call(functools.partial(denom_kernel, tiles), out_shape=f32(OH,...  2.2 us
  transfers between devices with their start and end apart: 8, of which 3 were waited for; matrix products, arithmetic and copies ran while one was open for 0% of the time, Pallas kernels for 11%

commit v1 on v0

--- a/solution.py
+++ b/solution.py
@@ -270,8 +270,8 @@
     core = lax.rem(lax.axis_index("mode"), 2)
     spots = positions.T
 
-    def along_x(array, steps):
-        return lax.ppermute(array, "mode", [(i, (i + 2 * steps) % modes) for i in range(modes)])
+    def along_x(array, flip):
+        return lax.ppermute(array, "mode", [(i, i ^ (2 * flip)) for i in range(modes)])
 
     def swap(array):
         return lax.ppermute(array, "mode", [(i, i ^ 1) for i in range(modes)])
@@ -285,7 +285,7 @@
                     pairs.append((source * modes + mode, tile * modes + mode))
         return lax.ppermute(array, ("tile", "mode"), pairs)
 
-    ring = [along_x(probe_modes, step) for step in (2, 1, -1)]
+    ring = [along_x(probe_modes, flip) for flip in (2, 3, 1)]
     edge, held = pl.pallas_call(
         pack_kernel,
         out_shape=(f32(2, OH, HALF), f32(MODES + 1, P_SIZE, P_SIZE)),

time: 63.3 us -> 62.8 us (level)
  the two profiles are of different devices: /device:TPU:257 before, /device:TPU:1 now
where the time goes in v1:
time: 62.8 us; the launch traced here: 62.1 us
  starting transfers between devices  27.7 us (44%)
  waiting for transfers between devices  26.8 us (43%)
  Pallas kernels  4.09 us (7%)
  local copies, waits for them, and re-layouts  2.15 us (3%)
  other arithmetic  1.1 us (2%)
    ppermute x3, waiting for transfers between devices, from_tile(): return lax.ppermute(array, ('tile', 'mode'), pairs)  12.2 us
    ppermute x3, starting transfers between devices, along_x(): lax.ppermute(array, 'mode', [(i, i ^ 2 * flip) for i in range(modes)])  10.2 us
    ppermute x2, starting transfers between devices, swap(): return lax.ppermute(array, 'mode', [(i, i ^ 1) for i in range(modes)])  9.86 us
    ppermute x3, waiting for transfers between devices, along_x(): lax.ppermute(array, 'mode', [(i, i ^ 2 * flip) for i in range(modes)])  9.83 us
    ppermute x3, starting transfers between devices, from_tile(): return lax.ppermute(array, ('tile', 'mode'), pairs)  7.72 us
    ppermute x2, waiting for transfers between devices, swap(): return lax.ppermute(array, 'mode', [(i, i ^ 1) for i in range(modes)])  4.75 us
    unnamed x12, local copies, waits for them, and re-layouts  2.15 us
    pallas_call x1, Pallas kernels, local(): pl.pallas_call(functools.partial(denom_kernel, tiles), out_shape=f32(OH,...  1.48 us
  transfers between devices with their start and end apart: 8, of which 4 were waited for; matrix products, arithmetic and copies ran while one was open for 0% of the time, Pallas kernels for 4%

profile of v1, /device:TPU:1, one launch (start us, length us, event | category | flops | bytes accessed | tf_op | source)
XLA Modules:
  0.0 62.1 jit_solution(7215744802094649228)
XLA Ops:
  0.0 5.5 %collective-permute-start.1 = (f32[1,2,256,256]{3,2,1,0:T(8,128)}, f32[1,2,256,256]{3,2,1,0:T(8,128)S(1)}, u32[]{:S(2)}, u32[]{:S(2)}) collective-permute-start(f32[1,2,256,256]{3,2,1,0:T(8,128)} %own.1), channel_id=1, source_target_pairs={{0,4},{1,5},{2,6},{3,7},{4,0},{5,1},{6,2},{7,3},{8,12},{9,13},{10,... | collective-permute-start | bytes 1572872 | tf_op jit(solution)/shard_map/ppermute | solution.py:274
  5.5 2.8 %collective-permute-start.2 = (f32[1,2,256,256]{3,2,1,0:T(8,128)}, f32[1,2,256,256]{3,2,1,0:T(8,128)S(1)}, u32[]{:S(2)}, u32[]{:S(2)}) collective-permute-start(f32[1,2,256,256]{3,2,1,0:T(8,128)} %own.1), channel_id=1, source_target_pairs={{0,6},{1,7},{2,4},{3,5},{4,2},{5,3},{6,0},{7,1},{8,14},{9,15},{10,... | collective-permute-start | bytes 1572872 | tf_op jit(solution)/shard_map/ppermute | solution.py:274
  8.3 1.9 %collective-permute-start.3 = (f32[1,2,256,256]{3,2,1,0:T(8,128)}, f32[1,2,256,256]{3,2,1,0:T(8,128)S(1)}, u32[]{:S(2)}, u32[]{:S(2)}) collective-permute-start(f32[1,2,256,256]{3,2,1,0:T(8,128)} %own.1), channel_id=1, source_target_pairs={{0,2},{1,3},{2,0},{3,1},{4,6},{5,7},{6,4},{7,5},{8,10},{9,11},{10,... | collective-permute-start | bytes 1572872 | tf_op jit(solution)/shard_map/ppermute | solution.py:274
  10.2 3.2 %collective-permute-start = (f32[2,256,256]{2,1,0:T(8,128)}, f32[2,256,256]{2,1,0:T(8,128)S(1)}, u32[]{:S(2)}, u32[]{:S(2)}) collective-permute-start(f32[2,256,256]{2,1,0:T(8,128)} %inten.1), channel_id=1, source_target_pairs={{8,0},{10,2},{12,4},{14,6},{16,8},{1,9},{18,10},{3,11},{20,12},{5,... | collective-permute-start | bytes 1572872 | tf_op jit(solution)/shard_map/ppermute | solution.py:286
  13.4 0.0 copy-start
  13.4 1.1 %copy-done = f32[2,320,256]{2,1,0:T(8,128)S(1)} copy-done((f32[2,320,256]{2,1,0:T(8,128)S(1)}, f32[2,320,256]{2,1,0:T(8,128)}, u32[]{:S(2)}) %copy-start) | copy-done | bytes 655384
  14.5 1.0 %copy-done.3 = f32[1,2,256,256]{3,2,1,0:T(8,128)S(1)} copy-done((f32[1,2,256,256]{3,2,1,0:T(8,128)S(1)}, f32[1,2,256,256]{3,2,1,0:T(8,128)}, u32[]{:S(2)}) %copy-start.3) | copy-done | bytes 524312
  15.6 0.1 pack.1
  15.6 3.2 %collective-permute-start.4 = (f32[2,320,128]{2,1,0:T(8,128)S(1)}, f32[2,320,128]{2,1,0:T(8,128)S(1)}, u32[]{:S(2)}, u32[]{:S(2)}) collective-permute-start(f32[2,320,128]{2,1,0:T(8,128)S(1)} %get-tuple-element.18), channel_id=1, source_target_pairs={{8,0},{10,2},{12,4},{14,6},{16,8},{1,9},{18,10},{3,11},{20,12},{5,... | collective-permute-start | bytes 983048 | tf_op jit(solution)/shard_map/ppermute | solution.py:286
  18.8 0.0 collective-permute-done.1.first
  18.9 9.8 %collective-permute-done.2.second = f32[1,2,256,256]{3,2,1,0:T(8,128)S(1)} collective-permute-done((f32[1,2,256,256]{3,2,1,0:T(8,128)}, f32[1,2,256,256]{3,2,1,0:T(8,128)S(1)}, u32[]{:S(2)}, u32[]{:S(2)}) %collective-permute-start.2) | collective-permute-done | bytes 524320 | tf_op jit(solution)/shard_map/ppermute | solution.py:274
  28.7 0.0 collective-permute-done.3.third
  28.7 0.1 merge.1.before
  28.8 0.0 copy-start.1
  28.8 0.0 copy-start.4
  28.9 0.0 copy-start.5
  28.9 0.0 collective-permute-done.inward
  28.9 0.0 copy-start.2
  28.9 0.0 collective-permute-done.4.beside
  28.9 7.5 %collective-permute-start.5 = (f32[9,256,256]{2,1,0:T(8,128)S(1)}, f32[9,256,256]{2,1,0:T(8,128)S(1)}, u32[]{:S(2)}, u32[]{:S(2)}) collective-permute-start(f32[9,256,256]{2,1,0:T(8,128)S(1)} %append.1.mine), channel_id=1, source_target_pairs={{0,1},{1,0},{2,3},{3,2},{4,5},{5,4},{6,7},{7,6},{8,9},{9,8},{10,11... | collective-permute-start | bytes 7077896 | tf_op jit(solution)/shard_map/ppermute | solution.py:277
  36.4 0.0 copy-done.1
  36.5 0.0 copy-done.4
  36.5 1.1 %far_of_own_modes.1 = (f32[3,2,256,256]{3,2,1,0:T(8,128)S(1)}, bf16[2,2,384,256]{3,2,1,0:T(8,128)(2,1)S(1)}, bf16[2,512,512]{2,1,0:T(8,128)(2,1)S(1)}, f32[3,4,256,512]{3,2,1,0:T(8,128)S(1)}, f32[3,256,256]{2,1,0:T(8,128)S(1)}) custom-call(s32[2,192]{1,0:T(2,128)S(1)} %bitcast.1, f32[2,129]{1,0:T(2,128)S(1)} %copy-done.5, f32[2,320,256]{2,1,0:T(8,128)S(1)} %copy-done.1, ...), custom_call_target="tpu_custom_call" | custom-call | bytes 21000000 | tf_op jit(solution)/shard_map/far_of_own_modes/pallas_call | solution.py:332
  37.5 3.0 %collective-permute-done.5.theirs = f32[9,256,256]{2,1,0:T(8,128)S(1)} collective-permute-done((f32[9,256,256]{2,1,0:T(8,128)S(1)}, f32[9,256,256]{2,1,0:T(8,128)S(1)}, u32[]{:S(2)}, u32[]{:S(2)}) %collective-permute-start.5) | collective-permute-done | bytes 2359328 | tf_op jit(solution)/shard_map/ppermute | solution.py:277
  40.6 1.3 %update_terms.1 = (f32[2,320,256]{2,1,0:T(8,128)S(1)}, f32[2,320,128]{2,1,0:T(8,128)S(1)}, f32[256,256]{1,0:T(8,128)S(1)}) custom-call(s32[2,192]{1,0:T(2,128)S(1)} %bitcast.2, f32[2,256,256]{2,1,0:T(8,128)S(1)} %copy-done.2, f32[2,256,256]{2,1,0:T(8,128)S(1)} %collective-permute-done.inward, f32[9,256,256]{2,1,0:T(8,128)S(1)} %append.1.mine, ...), custom_call_target="tpu_custom_call" | custom-call | bytes 35000000 | tf_op jit(solution)/shard_map/update_terms/pallas_call | solution.py:351
  41.9 1.3 %collective-permute-start.6 = (f32[2,320,128]{2,1,0:T(8,128)S(1)}, f32[2,320,128]{2,1,0:T(8,128)S(1)}, u32[]{:S(2)}, u32[]{:S(2)}) collective-permute-start(f32[2,320,128]{2,1,0:T(8,128)S(1)} %get-tuple-element.27), channel_id=1, source_target_pairs={{9,1},{11,3},{13,5},{15,7},{0,8},{17,9},{2,10},{19,11},{4,12},{21,... | collective-permute-start | bytes 983048 | tf_op jit(solution)/shard_map/ppermute | solution.py:286
  43.2 1.5 %denominator.1 = f32[320,256]{1,0:T(8,128)S(1)} custom-call(s32[2,192]{1,0:T(2,128)S(1)} %bitcast.3, f32[256,256]{1,0:T(8,128)S(1)} %get-tuple-element.28.weight), custom_call_target="tpu_custom_call" | custom-call | bytes 12250000 | tf_op jit(solution)/shard_map/denominator/pallas_call | solution.py:369
  44.7 12.2 %collective-permute-done.6 = f32[2,320,128]{2,1,0:T(8,128)S(1)} collective-permute-done((f32[2,320,128]{2,1,0:T(8,128)S(1)}, f32[2,320,128]{2,1,0:T(8,128)S(1)}, u32[]{:S(2)}, u32[]{:S(2)}) %collective-permute-start.6) | collective-permute-done | bytes 327712 | tf_op jit(solution)/shard_map/ppermute | solution.py:286
  56.9 0.1 fusion
  57.0 2.4 %collective-permute-start.7 = (f32[2,320,256]{2,1,0:T(8,128)S(1)}, f32[2,320,256]{2,1,0:T(8,128)S(1)}, u32[]{:S(2)}, u32[]{:S(2)}) collective-permute-start(f32[2,320,256]{2,1,0:T(8,128)S(1)} %fusion), channel_id=1, source_target_pairs={{0,1},{1,0},{2,3},{3,2},{4,5},{5,4},{6,7},{7,6},{8,9},{9,8},{10,11... | collective-permute-start | bytes 1966088 | tf_op jit(solution)/shard_map/ppermute | solution.py:277
  59.4 1.7 %collective-permute-done.7 = f32[2,320,256]{2,1,0:T(8,128)S(1)} collective-permute-done((f32[2,320,256]{2,1,0:T(8,128)S(1)}, f32[2,320,256]{2,1,0:T(8,128)S(1)}, u32[]{:S(2)}, u32[]{:S(2)}) %collective-permute-start.7) | collective-permute-done | bytes 655392 | tf_op jit(solution)/shard_map/ppermute | solution.py:277
  61.1 1.0 %add_add_fusion = f32[2,320,256]{2,1,0:T(8,128)} fusion(f32[2,320,256]{2,1,0:T(8,128)S(1)} %copy-done.1, f32[2,320,256]{2,1,0:T(8,128)S(1)} %fusion, f32[2,320,256]{2,1,0:T(8,128)S(1)} %collective-permute-done.7), kind=kLoop, calls=%fused_computation.2 | loop fusion | flops 327680 | bytes 2621440 | tf_op jit(solution)/shard_map/add | solution.py:383
  (5 shorter events, 0.1 us)
Async XLA Ops:
  0.0 18.8 %collective-permute-start.1 = (f32[1,2,256,256]{3,2,1,0:T(8,128)}, f32[1,2,256,256]{3,2,1,0:T(8,128)S(1)}, u32[]{:S(2)}, u32[]{:S(2)}) collective-permute-start(f32[1,2,256,256]{3,2,1,0:T(8,128)} %own.1), channel_id=1, source_target_pairs={{0,4},{1,5},{2,6},{3,7},{4,0},{5,1},{6,2},{7,3},{8,12},{9,13},{10,... | collective-permute-start | bytes 1572872 | tf_op jit(solution)/shard_map/ppermute | solution.py:274
  5.5 23.2 %collective-permute-start.2 = (f32[1,2,256,256]{3,2,1,0:T(8,128)}, f32[1,2,256,256]{3,2,1,0:T(8,128)S(1)}, u32[]{:S(2)}, u32[]{:S(2)}) collective-permute-start(f32[1,2,256,256]{3,2,1,0:T(8,128)} %own.1), channel_id=1, source_target_pairs={{0,6},{1,7},{2,4},{3,5},{4,2},{5,3},{6,0},{7,1},{8,14},{9,15},{10,... | collective-permute-start | bytes 1572872 | tf_op jit(solution)/shard_map/ppermute | solution.py:274
  8.3 20.4 %collective-permute-start.3 = (f32[1,2,256,256]{3,2,1,0:T(8,128)}, f32[1,2,256,256]{3,2,1,0:T(8,128)S(1)}, u32[]{:S(2)}, u32[]{:S(2)}) collective-permute-start(f32[1,2,256,256]{3,2,1,0:T(8,128)} %own.1), channel_id=1, source_target_pairs={{0,2},{1,3},{2,0},{3,1},{4,6},{5,7},{6,4},{7,5},{8,10},{9,11},{10,... | collective-permute-start | bytes 1572872 | tf_op jit(solution)/shard_map/ppermute | solution.py:274
  10.2 18.7 %collective-permute-start = (f32[2,256,256]{2,1,0:T(8,128)}, f32[2,256,256]{2,1,0:T(8,128)S(1)}, u32[]{:S(2)}, u32[]{:S(2)}) collective-permute-start(f32[2,256,256]{2,1,0:T(8,128)} %inten.1), channel_id=1, source_target_pairs={{8,0},{10,2},{12,4},{14,6},{16,8},{1,9},{18,10},{3,11},{20,12},{5,... | collective-permute-start | bytes 1572872 | tf_op jit(solution)/shard_map/ppermute | solution.py:286
  13.4 1.1 %copy-start = (f32[2,320,256]{2,1,0:T(8,128)S(1)}, f32[2,320,256]{2,1,0:T(8,128)}, u32[]{:S(2)}) copy-start(f32[2,320,256]{2,1,0:T(8,128)} %obj.3) | copy-start | bytes 1966084
  14.5 1.0 %copy-start.3 = (f32[1,2,256,256]{3,2,1,0:T(8,128)S(1)}, f32[1,2,256,256]{3,2,1,0:T(8,128)}, u32[]{:S(2)}) copy-start(f32[1,2,256,256]{3,2,1,0:T(8,128)} %own.1) | copy-start | bytes 1572868
  15.6 13.3 %collective-permute-start.4 = (f32[2,320,128]{2,1,0:T(8,128)S(1)}, f32[2,320,128]{2,1,0:T(8,128)S(1)}, u32[]{:S(2)}, u32[]{:S(2)}) collective-permute-start(f32[2,320,128]{2,1,0:T(8,128)S(1)} %get-tuple-element.18), channel_id=1, source_target_pairs={{8,0},{10,2},{12,4},{14,6},{16,8},{1,9},{18,10},{3,11},{20,12},{5,... | collective-permute-start | bytes 983048 | tf_op jit(solution)/shard_map/ppermute | solution.py:286
  28.8 7.6 %copy-start.1 = (f32[2,320,256]{2,1,0:T(8,128)S(1)}, f32[2,320,256]{2,1,0:T(8,128)}, u32[]{:S(2)}) copy-start(f32[2,320,256]{2,1,0:T(8,128)} %obj.3) | copy-start | bytes 1966084
  28.8 7.6 %copy-start.4 = (s32[192,2]{0,1:T(2,128)S(1)}, s32[192,2]{0,1:T(2,128)}, u32[]{:S(2)}) copy-start(s32[192,2]{0,1:T(2,128)} %param.6) | copy-start | bytes 4612
  28.9 7.6 %copy-start.5 = (f32[2,129]{1,0:T(2,128)S(1)}, f32[2,129]{1,0:T(2,128)}, u32[]{:S(2)}) copy-start(f32[2,129]{1,0:T(2,128)} %taps_ref.1) | copy-start | bytes 3100
  28.9 11.7 %copy-start.2 = (f32[2,256,256]{2,1,0:T(8,128)S(1)}, f32[2,256,256]{2,1,0:T(8,128)}, u32[]{:S(2)}) copy-start(f32[2,256,256]{2,1,0:T(8,128)} %inten.1) | copy-start | bytes 1572868
  28.9 11.6 %collective-permute-start.5 = (f32[9,256,256]{2,1,0:T(8,128)S(1)}, f32[9,256,256]{2,1,0:T(8,128)S(1)}, u32[]{:S(2)}, u32[]{:S(2)}) collective-permute-start(f32[9,256,256]{2,1,0:T(8,128)S(1)} %append.1.mine), channel_id=1, source_target_pairs={{0,1},{1,0},{2,3},{3,2},{4,5},{5,4},{6,7},{7,6},{8,9},{9,8},{10,11... | collective-permute-start | bytes 7077896 | tf_op jit(solution)/shard_map/ppermute | solution.py:277
  41.9 15.0 %collective-permute-start.6 = (f32[2,320,128]{2,1,0:T(8,128)S(1)}, f32[2,320,128]{2,1,0:T(8,128)S(1)}, u32[]{:S(2)}, u32[]{:S(2)}) collective-permute-start(f32[2,320,128]{2,1,0:T(8,128)S(1)} %get-tuple-element.27), channel_id=1, source_target_pairs={{9,1},{11,3},{13,5},{15,7},{0,8},{17,9},{2,10},{19,11},{4,12},{21,... | collective-permute-start | bytes 983048 | tf_op jit(solution)/shard_map/ppermute | solution.py:286
  57.0 4.1 %collective-permute-start.7 = (f32[2,320,256]{2,1,0:T(8,128)S(1)}, f32[2,320,256]{2,1,0:T(8,128)S(1)}, u32[]{:S(2)}, u32[]{:S(2)}) collective-permute-start(f32[2,320,256]{2,1,0:T(8,128)S(1)} %fusion), channel_id=1, source_target_pairs={{0,1},{1,0},{2,3},{3,2},{4,5},{5,4},{6,7},{7,6},{8,9},{9,8},{10,11... | collective-permute-start | bytes 1966088 | tf_op jit(solution)/shard_map/ppermute | solution.py:277
